TPU v7x, 128 devices: a whole 4x4x4 slice. The times are simulated.
128 devices in a mesh: expert: 64 (over y, z, x), half: 2 (over core).
Axes of the slice: x: 4, y: 4, z: 4, core: 2. Of those that a mesh axis runs over, the one named last changes fastest.
Arguments:
- hidden_in: bfloat16 [8192, 2048], P('expert'), may hold values from -6 to 6
- modality: int32 [8192], replicated, may hold values from 0 to 1, as said below
- expert_ids: int32 [8192, 8], P('expert'), may hold values from 0 to 63, all different within a row; in each aligned block of 128 rows (0 to 127, 128 to 255, ...) at most 24 rows name the same one
- route_weights: float32 [8192, 8], P('expert'), may hold values from 0.03 to 0.3
- w_gate_up: bfloat16 [128, 2048, 2, 768], P('expert', None, None, 'half'), may hold values from -0.125 to 0.125
- w_down: bfloat16 [128, 768, 2048], P('expert', 'half'), may hold values from -0.21875 to 0.21875
- norm_gain: float32 [2048], replicated, may hold values from 0.1 to 1.9
- w_query: bfloat16 [2048, 4096], P(None, 'half'), may hold values from -1 to 1
- key_value_weight: bfloat16 [2048, 2, 512], P(None, None, 'half'), may hold values from -1 to 1
- q_gain: float32 [128], replicated, may hold values from 1 to 8
- k_gain: float32 [128], replicated, may hold values from 1 to 8
Outputs:
- hidden_out: float32 [8192, 2048], P('expert')
- attended: bfloat16 [8192, 4096], P('expert', 'half')
Inputs may be any that keep to these rules, and one draw needn't show every extreme that they name: `modality`: constant over each aligned block of 128 tokens; both values occur. `expert_ids`: the 8 ids of a token differ; among the tokens of one aligned block of 128 no id is named more than 24 times, a bound that some block reaches.
All inputs are finite; a program needn't handle non-finite values.
Results may differ from a plain program's by a relative error of at most 0.03.
The roundings to bfloat16 on the way count: a program that leaves them out, or rounds other values in their place, can miss the bound.
Values may be sent and summed in bfloat16 or wider, within the bound.
A program may use at most 128 MiB of HBM per device.

v0:
```python
import math
import jax
import jax.numpy as jnp
from jax import lax
from jax.sharding import PartitionSpec as P

EPSILON = 1e-06


def from_partner(block, axis, stride):
    count = lax.axis_size(axis)
    route = []
    for low in range(count):
        high = low | 1 << stride
        if high != low and high < count:
            route += [(low, high), (high, low)]
    return lax.ppermute(block, axis, route)


def rms_scale(values, gain_row):
    mean_sq = jnp.mean(values * values, axis=-1, keepdims=True)
    return values * lax.rsqrt(mean_sq + EPSILON) * gain_row


def expert_pass(received, source_kind, w_gate_up, w_down):
    groups, slots, model_width = received.shape
    ordering = jnp.argsort(source_kind, stable=True)
    restore = jnp.argsort(ordering, stable=True)
    text_count = jnp.sum((source_kind == 0).astype(jnp.int32))
    group_sizes = jnp.stack([text_count * slots, (groups - text_count) * slots])
    rows_sorted = received[ordering].reshape(groups * slots, model_width)
    local_experts = w_gate_up.shape[0]
    half_units = w_gate_up.shape[3]
    gate_up = lax.ragged_dot(
        rows_sorted,
        w_gate_up.reshape(local_experts, model_width, 2 * half_units),
        group_sizes,
        preferred_element_type=jnp.float32,
    )
    activated = (jax.nn.silu(gate_up[:, :half_units]) * gate_up[:, half_units:]).astype(
        jnp.bfloat16
    )
    partial_out = lax.ragged_dot(activated, w_down, group_sizes, preferred_element_type=jnp.float32)
    return partial_out.reshape(groups, slots, model_width)[restore]


def body(
    hidden_in,
    modality,
    expert_ids,
    route_weights,
    w_gate_up,
    w_down,
    norm_gain,
    w_query,
    key_value_weight,
    q_gain,
    k_gain,
):
    tok_rows, model_width = hidden_in.shape
    top_count = expert_ids.shape[1]
    groups = lax.axis_size("expert")
    capacity = max(2, 3 * tok_rows * top_count // (2 * groups))
    source_kind = modality.reshape(groups, tok_rows)[:, 0]
    flat_ids = expert_ids.reshape(-1)
    row_total = tok_rows * top_count
    one_hot = (flat_ids[:, None] == jnp.arange(groups, dtype=jnp.int32)[None, :]).astype(jnp.int32)
    slot_rank = jnp.sum((jnp.cumsum(one_hot, axis=0) - one_hot) * one_hot, axis=1)
    slot_index = flat_ids * capacity + slot_rank
    row_token = jnp.arange(row_total, dtype=jnp.int32) // top_count
    slot_token = jnp.full((groups * capacity,), tok_rows, jnp.int32).at[slot_index].set(row_token)
    padded_in = jnp.concatenate([hidden_in, jnp.zeros((1, model_width), hidden_in.dtype)], axis=0)
    outgoing = padded_in[slot_token].reshape(groups, capacity, model_width)
    partial_out = expert_pass(
        lax.all_to_all(outgoing, "expert", split_axis=0, concat_axis=0, tiled=True),
        source_kind,
        w_gate_up,
        w_down,
    )
    combined = partial_out + from_partner(partial_out, "half", 0)
    returned = lax.all_to_all(
        combined.astype(jnp.bfloat16), "expert", split_axis=0, concat_axis=0, tiled=True
    )
    part_width = returned.shape[2]
    gathered = (
        returned.reshape(groups * capacity, part_width)[slot_index]
        .astype(jnp.float32)
        .reshape(tok_rows, top_count, part_width)
    )
    mixture = jnp.sum(gathered * route_weights[:, :, None], axis=1)
    hidden_out = hidden_in.astype(jnp.float32) + mixture
    normalized_input = rms_scale(hidden_out, norm_gain).astype(jnp.bfloat16)
    head_dim = q_gain.shape[0]
    queries = jnp.dot(normalized_input, w_query, preferred_element_type=jnp.float32)
    local_heads = queries.shape[1] // head_dim
    queries = rms_scale(queries.reshape(tok_rows, local_heads, head_dim), q_gain).astype(
        jnp.bfloat16
    )
    kv_width = key_value_weight.shape[2]
    kv_heads = kv_width // head_dim
    key_value_rows = jnp.dot(
        normalized_input,
        key_value_weight.reshape(model_width, 2 * kv_width),
        preferred_element_type=jnp.float32,
    ).reshape(tok_rows, 2, kv_heads, head_dim)
    keys_local = rms_scale(key_value_rows[:, 0], k_gain).astype(jnp.bfloat16)
    values_local = key_value_rows[:, 1].astype(jnp.bfloat16)
    stacked = jnp.stack([keys_local, values_local], axis=1).reshape(tok_rows, 2, kv_width)
    queries_per_group = local_heads // kv_heads
    query_rows = queries_per_group * tok_rows
    grouped_queries = (
        queries.reshape(tok_rows, kv_heads, queries_per_group, head_dim)
        .transpose(1, 2, 0, 3)
        .reshape(kv_heads, query_rows, head_dim)
    )
    score_scale = head_dim ** (-0.5)
    initial = (
        jnp.full((kv_heads, query_rows), -1e30, jnp.float32),
        jnp.zeros((kv_heads, query_rows), jnp.float32),
        jnp.zeros((kv_heads, query_rows, head_dim), jnp.float32),
    )
    kv_piece = lax.all_gather(stacked, "expert", axis=0, tiled=True)
    key_rows = kv_piece.shape[0]
    key_block = math.gcd(key_rows, 1024)
    blocks = kv_piece.reshape(key_rows // key_block, key_block, 2, kv_heads, head_dim)

    def step_block(inner_state, kv_block):
        peak_in, totals_in, accum_in = inner_state
        scores = (
            jnp.einsum(
                "hrd,khd->hrk", grouped_queries, kv_block[:, 0], preferred_element_type=jnp.float32
            )
            * score_scale
        )
        new_peak = jnp.maximum(peak_in, jnp.max(scores, axis=-1))
        weights = jnp.exp(scores - new_peak[..., None])
        rescale = jnp.exp(peak_in - new_peak)
        totals_out = totals_in * rescale + jnp.sum(weights, axis=-1)
        accum_out = accum_in * rescale[..., None] + jnp.einsum(
            "hrk,khd->hrd",
            weights.astype(jnp.bfloat16),
            kv_block[:, 1],
            preferred_element_type=jnp.float32,
        )
        return ((new_peak, totals_out, accum_out), None)

    final_state = lax.scan(step_block, initial, blocks)[0]
    accumulated = final_state[2] / final_state[1][..., None]
    attended = (
        accumulated.reshape(kv_heads, queries_per_group, tok_rows, head_dim)
        .transpose(2, 0, 1, 3)
        .reshape(tok_rows, local_heads * head_dim)
        .astype(jnp.bfloat16)
    )
    return (hidden_out, attended)


def solution(mesh):
    in_specs = (
        P("expert", None),
        P(),
        P("expert", None),
        P("expert", None),
        P("expert", None, None, "half"),
        P("expert", "half", None),
        P(),
        P(None, "half"),
        P(None, None, "half"),
        P(),
        P(),
    )
    out_specs = (P("expert", None), P("expert", "half"))
    return jax.shard_map(body, mesh=mesh, in_specs=in_specs, out_specs=out_specs, check_vma=False)
```

profile of v0, /device:TPU:0, one launch (start us, length us, event | category | flops | bytes accessed | tf_op | source)
XLA Modules:
  0.0 562.9 jit_solution(2645386171560433740)
XLA Ops:
  8.9 18.0 %reduce-window.6 = s32[64,8,128]{2,1,0:T(8,128)S(1)} reduce-window(s32[64,8,128]{2,1,0:T(8,128)S(1)} %fusion.22, s32[]{:T(128)} %constant.32.clone.1), window={size=1x1x128 pad=0_0x0_0x127_0}, to_apply=%region_0.0 | reduce-window | flops 8323072 | bytes 524292 | tf_op jit(solution)/shard_map/reduce-window
  27.7 4.3 scatter_custom_fusion
  32.1 1.1 concatenate.4
  33.2 7.1 %gather_fusion = bf16[1536,2048]{1,0:T(8,128)(2,1)} fusion(bf16[129,2048]{1,0:T(8,128)(2,1)S(1)} %concatenate.4, s32[2048]{0:T(1024)S(1)} %pad_clamp_fusion), kind=kCustom, calls=%fused_computation | custom fusion | bytes 12589056 | tf_op jit(solution)/shard_map/gather | solution.py:73
  40.3 11.9 %all-to-all-start = ((bf16[64,24,2048]{2,1,0:T(8,128)(2,1)}), bf16[64,24,2048]{2,1,0:T(8,128)(2,1)}, u32[]{:S(2)}, u32[]{:S(2)}) async-start(bf16[64,24,2048]{2,1,0:T(8,128)(2,1)} %bitcast.107), calls=%async_computation | async-start | bytes 12582912 | tf_op jit(solution)/shard_map/all_to_all | solution.py:75
  52.3 2.0 sort.31
  56.8 1.3 ragged-dot-metadata
  58.2 14.6 %reshape.140 = bf16[2,2048,768]{2,1,0:T(8,128)(2,1)} reshape(bf16[2,2048,2,384]{3,2,1,0:T(2,128)(2,1)} %param.17) | data formatting | bytes 12582912 | tf_op jit(solution)/shard_map/reshape | solution.py:36
  72.8 2.0 sort.32
  74.8 57.0 %all-to-all-done = bf16[64,24,2048]{2,1,0:T(8,128)(2,1)} async-done(((bf16[64,24,2048]{2,1,0:T(8,128)(2,1)}), bf16[64,24,2048]{2,1,0:T(8,128)(2,1)}, u32[]{:S(2)}, u32[]{:S(2)}) %all-to-all-start) | async-done | bytes 6291488 | tf_op jit(solution)/shard_map/all_to_all | solution.py:75
  131.9 6.4 %gather_fusion.1 = bf16[64,24,2048]{2,1,0:T(8,128)(2,1)} fusion(bf16[64,24,2048]{2,1,0:T(8,128)(2,1)} %all-to-all-done, s32[1024]{0:T(1024)S(1)} %pad_clamp_fusion.2), kind=kCustom, calls=%fused_computation.1 | custom fusion | bytes 12583168 | tf_op jit(solution)/shard_map/gather | solution.py:31
  138.2 13.9 %ragged-dot-none.1 = f32[1536,768]{1,0:T(8,128)} custom-call(s32[1]{0:T(128)} %get-tuple-element.41, s32[3]{0:T(128)} %get-tuple-element.42, s32[7]{0:T(128)} %get-tuple-element.43, s32[7]{0:T(128)} %get-tuple-element.44, s32[1]{0:T(128)} %get-tuple-element.41, bf16[1536,2048]{1,0:T(8,128)(2,1)} %bitcast.113, bf16[2,2048,768]{2,1,0:T(8,128)(2,1)} %reshape.140), custom_call_target="tpu_custom_call" | custom-call | flops 4831838208 | bytes 17301512 | tf_op jit(solution)/shard_map/ragged_dot_general/ragged-dot-none
  152.1 4.1 fusion.15
  156.2 12.3 %ragged-dot-none = f32[1536,2048]{1,0:T(8,128)} custom-call(s32[1]{0:T(128)} %get-tuple-element.41, s32[3]{0:T(128)} %get-tuple-element.42, s32[7]{0:T(128)} %get-tuple-element.43, s32[7]{0:T(128)} %get-tuple-element.44, s32[1]{0:T(128)} %get-tuple-element.41, bf16[1536,384]{1,0:T(8,128)(2,1)} %fusion.15, bf16[2,384,2048]{2,1,0:T(8,128)(2,1)} %param.18), custom_call_target="tpu_custom_call" | custom-call | flops 2415919104 | bytes 16908296 | tf_op jit(solution)/shard_map/ragged_dot_general/ragged-dot-none
  168.5 10.4 %gather_fusion.2 = f32[64,24,2048]{2,1,0:T(8,128)} fusion(f32[64,24,2048]{2,1,0:T(8,128)} %bitcast.105, s32[1024]{0:T(1024)S(1)} %pad_clamp_fusion.1), kind=kCustom, calls=%fused_computation.2 | custom fusion | bytes 25166080 | tf_op jit(solution)/shard_map/gather | solution.py:44
  178.9 19.4 %collective-permute-done = f32[64,24,2048]{2,1,0:T(8,128)S(1)} collective-permute-done((f32[64,24,2048]{2,1,0:T(8,128)}, f32[64,24,2048]{2,1,0:T(8,128)S(1)}, u32[]{:S(2)}, u32[]{:S(2)}) %collective-permute-start) | collective-permute-done | bytes 12582944 | tf_op jit(solution)/shard_map/ppermute | solution.py:17
  198.3 8.5 %add_convert_fusion = bf16[64,24,2048]{2,1,0:T(8,128)(2,1)} fusion(f32[64,24,2048]{2,1,0:T(8,128)} %gather_fusion.2, f32[64,24,2048]{2,1,0:T(8,128)S(1)} %collective-permute-done), kind=kLoop, calls=%fused_computation.25 | loop fusion | flops 6291456 | bytes 31457280 | tf_op jit(solution)/shard_map/convert_element_type | solution.py:82
  206.8 7.7 %all-to-all-start.1 = ((bf16[64,24,2048]{2,1,0:T(8,128)(2,1)}), bf16[64,24,2048]{2,1,0:T(8,128)(2,1)}, u32[]{:S(2)}, u32[]{:S(2)}) async-start(bf16[64,24,2048]{2,1,0:T(8,128)(2,1)} %add_convert_fusion), calls=%async_computation.1 | async-start | bytes 12582912 | tf_op jit(solution)/shard_map/all_to_all | solution.py:81
  214.5 10.4 %all-gather.2.cloned.1.call-start = ((), (), s32[]{:S(2)}) async-start(), calls=%async_computation.2 | async-start | bytes 8519680 | tf_op jit(solution)/shard_map/all_gather | solution.py:122
  225.0 2.0 copy.71
  227.1 2.5 copy.62
  229.5 66.1 %all-to-all-done.1 = bf16[64,24,2048]{2,1,0:T(8,128)(2,1)} async-done(((bf16[64,24,2048]{2,1,0:T(8,128)(2,1)}), bf16[64,24,2048]{2,1,0:T(8,128)(2,1)}, u32[]{:S(2)}, u32[]{:S(2)}) %all-to-all-start.1) | async-done | bytes 6291488 | tf_op jit(solution)/shard_map/all_to_all | solution.py:81
  295.7 12.5 %gather_fusion.3 = bf16[1024,2048]{1,0:T(8,128)(2,1)} fusion(bf16[1536,2048]{1,0:T(8,128)(2,1)} %bitcast.10, s32[1024]{0:T(1024)S(1)} %broadcast_clamp_fusion), kind=kCustom, calls=%fused_computation.3 | custom fusion | bytes 8392704 | tf_op jit(solution)/shard_map/gather | solution.py:86
  308.2 6.7 %fusion.14 = f32[128,2048]{1,0:T(8,128)S(1)} fusion(bf16[1024,2048]{1,0:T(8,128)(2,1)} %gather_fusion.3, f32[128,8]{1,0:T(8,128)S(1)} %copy.61), kind=kLoop, calls=%fused_computation.27 | loop fusion | flops 6029312 | bytes 5246976 | tf_op jit(solution)/shard_map/reduce_sum | solution.py:90
  316.8 4.7 fusion.29
  323.1 90.7 %all-gather.2.cloned.1.call-done = bf16[8192,2,256]{0,2,1:T(8,128)(2,1)} async-done(((bf16[128,2,256]{0,2,1:T(8,128)(2,1)}), bf16[8192,2,256]{0,2,1:T(8,128)(2,1)}) %all-gather.2.cloned.1.call-update) | async-done | bytes 8388624 | tf_op jit(solution)/shard_map/all_gather | solution.py:122
  413.8 16.5 %copy.72 = bf16[64,8,8,1024]{3,2,1,0:T(8,128)(2,1)} copy(bf16[64,8,8,1024]{3,1,2,0:T(8,128)(2,1)} %bitcast.110) | data formatting | bytes 16777216
  430.3 12.0 %copy.66 = bf16[8,1024,2,2,128]{4,1,3,2,0:T(8,128)(2,1)} copy(bf16[8,1024,2,2,128]{1,0,4,3,2:T(8,128)(2,1)} %bitcast.106) | data formatting | bytes 16777216
  442.3 111.7 %while.15 = (s32[]{:T(128)}, f32[2,1024]{1,0:T(2,128)S(1)}, f32[2,1024]{1,0:T(2,128)S(1)}, f32[2,1024,128]{2,1,0:T(8,128)S(1)}, bf16[8,1024,2,2,128]{4,1,3,2,0:T...) while((s32[]{:T(128)}, f32[2,1024]{1,0:T(2,128)S(1)}, ...), condition=%wide.region_14.15_spmd.clone, body=%wide.region_11.14_spmd.clone.sunk | while | flops 1091315712 | bytes 64618624 | solution.py:147
  442.3 1.3 dynamic-slice_bitcast_fusion.2
  443.6 4.5 bitcast_reduce_fusion.2
  448.1 4.9 fusion.42
  453.0 0.8 copy-done
  453.8 2.4 fusion.44
  456.2 1.3 dynamic-slice_bitcast_fusion.2
  457.6 4.5 bitcast_reduce_fusion.2
  462.0 4.9 fusion.42
  467.8 2.4 fusion.44
  470.2 1.3 dynamic-slice_bitcast_fusion.2
  471.5 4.5 bitcast_reduce_fusion.2
  476.0 4.9 fusion.42
  481.0 0.8 copy-done
  481.8 2.4 fusion.44
  484.2 1.3 dynamic-slice_bitcast_fusion.2
  485.5 4.5 bitcast_reduce_fusion.2
  490.0 4.9 fusion.42
  495.7 2.4 fusion.44
  498.2 1.3 dynamic-slice_bitcast_fusion.2
  499.5 4.5 bitcast_reduce_fusion.2
  503.9 4.9 fusion.42
  509.7 2.4 fusion.44
  512.1 1.3 dynamic-slice_bitcast_fusion.2
  513.4 4.5 bitcast_reduce_fusion.2
  517.9 4.9 fusion.42
  523.7 2.4 fusion.44
  526.1 1.3 dynamic-slice_bitcast_fusion.2
  527.4 4.5 bitcast_reduce_fusion.2
  531.9 4.9 fusion.42
  537.6 2.4 fusion.44
  540.1 1.3 dynamic-slice_bitcast_fusion.2
  541.4 4.5 bitcast_reduce_fusion.2
  545.8 4.9 fusion.42
  551.6 2.4 fusion.44
  554.7 0.9 copy.78
  (107 shorter events, 13.3 us)
Async XLA Ops:
  40.3 11.9 %copy-start.5 = (s32[8192]{0:T(1024)S(1)}, s32[8192]{0:T(1024)}, u32[]{:S(2)}) copy-start(s32[8192]{0:T(1024)} %param.14) | copy-start | bytes 98308
  40.3 91.6 %all-to-all-start = ((bf16[64,24,2048]{2,1,0:T(8,128)(2,1)}), bf16[64,24,2048]{2,1,0:T(8,128)(2,1)}, u32[]{:S(2)}, u32[]{:S(2)}) async-start(bf16[64,24,2048]{2,1,0:T(8,128)(2,1)} %bitcast.107), calls=%async_computation | async-start | bytes 12582912 | tf_op jit(solution)/shard_map/all_to_all | solution.py:75
  178.9 19.4 %collective-permute-start = (f32[64,24,2048]{2,1,0:T(8,128)}, f32[64,24,2048]{2,1,0:T(8,128)S(1)}, u32[]{:S(2)}, u32[]{:S(2)}) collective-permute-start(f32[64,24,2048]{2,1,0:T(8,128)} %gather_fusion.2), channel_id=1, source_target_pairs={{0,1},{1,0},{2,3},{3,2},{4,5},{5,4},{6,7},{7,6},{8,9},{9,8},{10,11... | collective-permute-start | bytes 37748744 | tf_op jit(solution)/shard_map/ppermute | solution.py:17
  206.8 18.1 %copy-start.6 = (f32[128,8]{0,1:T(8,128)S(1)}, f32[128,8]{0,1:T(8,128)}, u32[]{:S(2)}) copy-start(f32[128,8]{0,1:T(8,128)} %param.16) | copy-start | bytes 12292
  206.8 88.9 %all-to-all-start.1 = ((bf16[64,24,2048]{2,1,0:T(8,128)(2,1)}), bf16[64,24,2048]{2,1,0:T(8,128)(2,1)}, u32[]{:S(2)}, u32[]{:S(2)}) async-start(bf16[64,24,2048]{2,1,0:T(8,128)(2,1)} %add_convert_fusion), calls=%async_computation.1 | async-start | bytes 12582912 | tf_op jit(solution)/shard_map/all_to_all | solution.py:81
  214.5 199.3 %all-gather.2.cloned.1.call-start = ((), (), s32[]{:S(2)}) async-start(), calls=%async_computation.2 | async-start | bytes 8519680 | tf_op jit(solution)/shard_map/all_gather | solution.py:122
  295.7 19.1 %copy-start.3 = (bf16[128,2048]{1,0:T(8,128)(2,1)S(1)}, bf16[128,2048]{1,0:T(8,128)(2,1)}, u32[]{:S(2)}) copy-start(bf16[128,2048]{1,0:T(8,128)(2,1)} %param.13) | copy-start | bytes 1572868
  308.2 6.9 %copy-start.2 = (bf16[512,2048]{1,0:T(8,128)(2,1)S(1)}, bf16[512,2048]{1,0:T(8,128)(2,1)}, u32[]{:S(2)}) copy-start(bf16[512,2048]{1,0:T(8,128)(2,1)} %copy.62) | copy-start | bytes 6291460
  308.2 7.0 %copy-start.4 = (f32[2048]{0:T(1024)S(1)}, f32[2048]{0:T(1024)}, u32[]{:S(2)}) copy-start(f32[2048]{0:T(1024)} %param.19) | copy-start | bytes 24580
  308.2 7.8 %copy-start.8 = (f32[128]{0:T(128)S(1)}, f32[128]{0:T(128)}, u32[]{:S(2)}) copy-start(f32[128]{0:T(128)} %param.23) | copy-start | bytes 1540
  315.1 6.4 %copy-start.1 = (f32[128,2048]{1,0:T(8,128)}, f32[128,2048]{1,0:T(8,128)S(1)}, u32[]{:S(2)}) copy-start(f32[128,2048]{1,0:T(8,128)S(1)} %get-tuple-element.109) | copy-start | bytes 3145732
  321.5 1.1 copy-start.7
  448.1 5.8 %copy-start = (f32[2,1024,1024]{2,1,0:T(8,128)S(1)}, f32[2,1024,1024]{2,1,0:T(8,128)}, u32[]{:S(2)}) copy-start(f32[2,1024,1024]{2,1,0:T(8,128)} %get-tuple-element.154) | copy-start | bytes 25165828 | tf_op jit(solution)/shard_map/while
  462.0 5.8 %copy-start = (f32[2,1024,1024]{2,1,0:T(8,128)S(1)}, f32[2,1024,1024]{2,1,0:T(8,128)}, u32[]{:S(2)}) copy-start(f32[2,1024,1024]{2,1,0:T(8,128)} %get-tuple-element.154) | copy-start | bytes 25165828 | tf_op jit(solution)/shard_map/while
  476.0 5.8 %copy-start = (f32[2,1024,1024]{2,1,0:T(8,128)S(1)}, f32[2,1024,1024]{2,1,0:T(8,128)}, u32[]{:S(2)}) copy-start(f32[2,1024,1024]{2,1,0:T(8,128)} %get-tuple-element.154) | copy-start | bytes 25165828 | tf_op jit(solution)/shard_map/while
  490.0 5.8 %copy-start = (f32[2,1024,1024]{2,1,0:T(8,128)S(1)}, f32[2,1024,1024]{2,1,0:T(8,128)}, u32[]{:S(2)}) copy-start(f32[2,1024,1024]{2,1,0:T(8,128)} %get-tuple-element.154) | copy-start | bytes 25165828 | tf_op jit(solution)/shard_map/while
  503.9 5.8 %copy-start = (f32[2,1024,1024]{2,1,0:T(8,128)S(1)}, f32[2,1024,1024]{2,1,0:T(8,128)}, u32[]{:S(2)}) copy-start(f32[2,1024,1024]{2,1,0:T(8,128)} %get-tuple-element.154) | copy-start | bytes 25165828 | tf_op jit(solution)/shard_map/while
  517.9 5.8 %copy-start = (f32[2,1024,1024]{2,1,0:T(8,128)S(1)}, f32[2,1024,1024]{2,1,0:T(8,128)}, u32[]{:S(2)}) copy-start(f32[2,1024,1024]{2,1,0:T(8,128)} %get-tuple-element.154) | copy-start | bytes 25165828 | tf_op jit(solution)/shard_map/while
  531.9 5.8 %copy-start = (f32[2,1024,1024]{2,1,0:T(8,128)S(1)}, f32[2,1024,1024]{2,1,0:T(8,128)}, u32[]{:S(2)}) copy-start(f32[2,1024,1024]{2,1,0:T(8,128)} %get-tuple-element.154) | copy-start | bytes 25165828 | tf_op jit(solution)/shard_map/while
  545.8 5.8 %copy-start = (f32[2,1024,1024]{2,1,0:T(8,128)S(1)}, f32[2,1024,1024]{2,1,0:T(8,128)}, u32[]{:S(2)}) copy-start(f32[2,1024,1024]{2,1,0:T(8,128)} %get-tuple-element.154) | copy-start | bytes 25165828 | tf_op jit(solution)/shard_map/while
Sparse Core Ops, SparseCore 0:
  316.9 96.8 all-gather.1
where the time goes:
time: 573 us; the launch traced here: 563 us
  waiting for transfers between devices  233 us (41%)
  local copies, waits for them, and re-layouts  110 us (19%)
  other arithmetic  85.3 us (15%)
  matrix products  60.3 us (11%)
  starting transfers between devices  30 us (5%)
  Pallas kernels  27.5 us (5%)
  between operations  16.1 us (3%)
    all_gather x1, waiting for transfers between devices, body(): kv_piece = lax.all_gather(stacked, 'expert', axis=0, tiled=True)  90.7 us
    all_to_all x1, waiting for transfers between devices, body(): lax.all_to_all(combined.astype(jnp.bfloat16), 'expert', split_axis=0, con...  66.1 us
    all_to_all x1, waiting for transfers between devices, body(): lax.all_to_all(outgoing, 'expert', split_axis=0, concat_axis=0, tiled=True)  57 us
    reduce_sum x8, other arithmetic, step_block(): totals_out = totals_in * rescale + jnp.sum(weights, axis=-1)  39.3 us
    dot_general x8, matrix products, step_block(): jnp.einsum('hrd,khd->hrk', grouped_queries, kv_block[:, 0], preferred_ele...  35.7 us
    unnamed x24, local copies, waits for them, and re-layouts  32.8 us
    another operation x2, Pallas kernels  26.2 us
    ppermute x1, waiting for transfers between devices, from_partner(): return lax.ppermute(block, axis, route)  19.4 us
  transfers between devices with their start and end apart: 4, of which 4 were waited for; matrix products, arithmetic and copies ran while one was open for 5% of the time, Pallas kernels for 0%

commit v1 on v0

--- a/solution.py
+++ b/solution.py
@@ -119,7 +119,9 @@
         jnp.zeros((kv_heads, query_rows), jnp.float32),
         jnp.zeros((kv_heads, query_rows, head_dim), jnp.float32),
     )
-    kv_piece = lax.all_gather(stacked, "expert", axis=0, tiled=True)
+    kv_piece = jnp.concatenate(
+        lax.all_to_all(jnp.stack([stacked] * lax.axis_size("expert")), "expert", 0, 0), axis=0
+    )
     key_rows = kv_piece.shape[0]
     key_block = math.gcd(key_rows, 1024)
     blocks = kv_piece.reshape(key_rows // key_block, key_block, 2, kv_heads, head_dim)

time: 573 us -> 587 us (1.024)
  waiting for transfers between devices: 233 us -> 255 us
  local copies, waits for them, and re-layouts: 110 us -> 124 us
  between operations: 16.1 us -> 2.32 us
    all_to_all x0 -> x1, waiting for transfers between devices: none -> 102 us  [body(): lax.all_to_all(jnp.stack([stacked] * lax.axis_size('expert')), 'expert',...]
    all_gather x1 -> x0, waiting for transfers between devices: 90.7 us -> none  [body(): kv_piece = lax.all_gather(stacked, 'expert', axis=0, tiled=True)]
    another operation x2 -> x4, local copies, waits for them, and re-layouts: 0.09 us -> 18.7 us  [the longest x1 13.3 us: body(): kv_piece.reshape(key_rows // key_block, key_block, 2, kv_heads, head_dim)]
    unnamed x24 -> x23, local copies, waits for them, and re-layouts: 32.8 us -> 16.3 us
    all_to_all x0 -> x1, local copies, waits for them, and re-layouts: none -> 12 us  [body(): lax.all_to_all(jnp.stack([stacked] * lax.axis_size('expert')), 'expert',...]
    all_gather x1 -> x0, starting transfers between devices: 10.4 us -> none  [body(): kv_piece = lax.all_gather(stacked, 'expert', axis=0, tiled=True)]
    all_to_all x1, waiting for transfers between devices: 66.1 us -> 76.4 us  [body(): lax.all_to_all(combined.astype(jnp.bfloat16), 'expert', split_axis=0, con...]
    all_to_all x0 -> x1, starting transfers between devices: none -> 8.07 us  [body(): lax.all_to_all(jnp.stack([stacked] * lax.axis_size('expert')), 'expert',...]
where the time goes in v1:
time: 587 us; the launch traced here: 582 us
  waiting for transfers between devices  255 us (43%)
  local copies, waits for them, and re-layouts  124 us (21%)
  other arithmetic  84.6 us (14%)
  matrix products  60.3 us (10%)
  starting transfers between devices  27.8 us (5%)
  Pallas kernels  27.5 us (5%)
    all_to_all x1, waiting for transfers between devices, body(): lax.all_to_all(jnp.stack([stacked] * lax.axis_size('expert')), 'expert',...  102 us
    all_to_all x1, waiting for transfers between devices, body(): lax.all_to_all(combined.astype(jnp.bfloat16), 'expert', split_axis=0, con...  76.4 us
    all_to_all x1, waiting for transfers between devices, body(): lax.all_to_all(outgoing, 'expert', split_axis=0, concat_axis=0, tiled=True)  57 us
    reduce_sum x8, other arithmetic, step_block(): totals_out = totals_in * rescale + jnp.sum(weights, axis=-1)  39.3 us
    dot_general x8, matrix products, step_block(): jnp.einsum('hrd,khd->hrk', grouped_queries, kv_block[:, 0], preferred_ele...  35.7 us
    another operation x2, Pallas kernels  26.2 us
    ppermute x1, waiting for transfers between devices, from_partner(): return lax.ppermute(block, axis, route)  19.4 us
    dot_general x8, matrix products, step_block(): jnp.einsum('hrk,khd->hrd', weights.astype(jnp.bfloat16), kv_block[:, 1],...  19.1 us
  transfers between devices with their start and end apart: 4, of which 4 were waited for; matrix products, arithmetic and copies ran while one was open for 5% of the time, Pallas kernels for 0%

profile of v1, /device:TPU:0, one launch (start us, length us, event | category | flops | bytes accessed | tf_op | source)
XLA Modules:
  0.0 582.3 jit_solution(15908903539385611907)
XLA Ops:
  2.3 18.0 %reduce-window.6 = s32[64,8,128]{2,1,0:T(8,128)S(1)} reduce-window(s32[64,8,128]{2,1,0:T(8,128)S(1)} %fusion.22, s32[]{:T(128)} %constant.32.clone.1), window={size=1x1x128 pad=0_0x0_0x127_0}, to_apply=%region_0.0 | reduce-window | flops 8323072 | bytes 524292 | tf_op jit(solution)/shard_map/reduce-window
  21.2 4.3 scatter_custom_fusion
  25.5 1.1 concatenate.4
  26.6 7.1 %gather_fusion = bf16[1536,2048]{1,0:T(8,128)(2,1)} fusion(bf16[129,2048]{1,0:T(8,128)(2,1)S(1)} %concatenate.4, s32[2048]{0:T(1024)S(1)} %pad_clamp_fusion), kind=kCustom, calls=%fused_computation | custom fusion | bytes 12589056 | tf_op jit(solution)/shard_map/gather | solution.py:73
  33.7 11.9 %all-to-all-start = ((bf16[64,24,2048]{2,1,0:T(8,128)(2,1)}), bf16[64,24,2048]{2,1,0:T(8,128)(2,1)}, u32[]{:S(2)}, u32[]{:S(2)}) async-start(bf16[64,24,2048]{2,1,0:T(8,128)(2,1)} %bitcast.106), calls=%async_computation | async-start | bytes 12582912 | tf_op jit(solution)/shard_map/all_to_all | solution.py:75
  45.7 2.0 sort.31
  50.3 1.3 ragged-dot-metadata
  51.6 14.6 %reshape.137 = bf16[2,2048,768]{2,1,0:T(8,128)(2,1)} reshape(bf16[2,2048,2,384]{3,2,1,0:T(2,128)(2,1)} %param.17) | data formatting | bytes 12582912 | tf_op jit(solution)/shard_map/reshape | solution.py:36
  66.2 2.0 sort.32
  68.3 57.0 %all-to-all-done = bf16[64,24,2048]{2,1,0:T(8,128)(2,1)} async-done(((bf16[64,24,2048]{2,1,0:T(8,128)(2,1)}), bf16[64,24,2048]{2,1,0:T(8,128)(2,1)}, u32[]{:S(2)}, u32[]{:S(2)}) %all-to-all-start) | async-done | bytes 6291488 | tf_op jit(solution)/shard_map/all_to_all | solution.py:75
  125.3 6.4 %gather_fusion.1 = bf16[64,24,2048]{2,1,0:T(8,128)(2,1)} fusion(bf16[64,24,2048]{2,1,0:T(8,128)(2,1)} %all-to-all-done, s32[1024]{0:T(1024)S(1)} %pad_clamp_fusion.2), kind=kCustom, calls=%fused_computation.1 | custom fusion | bytes 12583168 | tf_op jit(solution)/shard_map/gather | solution.py:31
  131.7 13.9 %ragged-dot-none.1 = f32[1536,768]{1,0:T(8,128)} custom-call(s32[1]{0:T(128)} %get-tuple-element.41, s32[3]{0:T(128)} %get-tuple-element.42, s32[7]{0:T(128)} %get-tuple-element.43, s32[7]{0:T(128)} %get-tuple-element.44, s32[1]{0:T(128)} %get-tuple-element.41, bf16[1536,2048]{1,0:T(8,128)(2,1)} %bitcast.111, bf16[2,2048,768]{2,1,0:T(8,128)(2,1)} %reshape.137), custom_call_target="tpu_custom_call" | custom-call | flops 4831838208 | bytes 17301512 | tf_op jit(solution)/shard_map/ragged_dot_general/ragged-dot-none
  145.6 4.1 fusion.15
  149.7 12.3 %ragged-dot-none = f32[1536,2048]{1,0:T(8,128)} custom-call(s32[1]{0:T(128)} %get-tuple-element.41, s32[3]{0:T(128)} %get-tuple-element.42, s32[7]{0:T(128)} %get-tuple-element.43, s32[7]{0:T(128)} %get-tuple-element.44, s32[1]{0:T(128)} %get-tuple-element.41, bf16[1536,384]{1,0:T(8,128)(2,1)} %fusion.15, bf16[2,384,2048]{2,1,0:T(8,128)(2,1)} %param.18), custom_call_target="tpu_custom_call" | custom-call | flops 2415919104 | bytes 16908296 | tf_op jit(solution)/shard_map/ragged_dot_general/ragged-dot-none
  162.0 10.4 %gather_fusion.2 = f32[64,24,2048]{2,1,0:T(8,128)} fusion(f32[64,24,2048]{2,1,0:T(8,128)} %bitcast.105, s32[1024]{0:T(1024)S(1)} %pad_clamp_fusion.1), kind=kCustom, calls=%fused_computation.2 | custom fusion | bytes 25166080 | tf_op jit(solution)/shard_map/gather | solution.py:44
  172.4 19.4 %collective-permute-done = f32[64,24,2048]{2,1,0:T(8,128)S(1)} collective-permute-done((f32[64,24,2048]{2,1,0:T(8,128)}, f32[64,24,2048]{2,1,0:T(8,128)S(1)}, u32[]{:S(2)}, u32[]{:S(2)}) %collective-permute-start) | collective-permute-done | bytes 12582944 | tf_op jit(solution)/shard_map/ppermute | solution.py:17
  191.8 8.5 %add_convert_fusion = bf16[64,24,2048]{2,1,0:T(8,128)(2,1)} fusion(f32[64,24,2048]{2,1,0:T(8,128)} %gather_fusion.2, f32[64,24,2048]{2,1,0:T(8,128)S(1)} %collective-permute-done), kind=kLoop, calls=%fused_computation.25 | loop fusion | flops 6291456 | bytes 31457280 | tf_op jit(solution)/shard_map/convert_element_type | solution.py:82
  200.3 7.8 %all-to-all-start.1 = ((bf16[64,24,2048]{2,1,0:T(8,128)(2,1)}), bf16[64,24,2048]{2,1,0:T(8,128)(2,1)}, u32[]{:S(2)}, u32[]{:S(2)}) async-start(bf16[64,24,2048]{2,1,0:T(8,128)(2,1)} %add_convert_fusion), calls=%async_computation.1 | async-start | bytes 12582912 | tf_op jit(solution)/shard_map/all_to_all | solution.py:81
  208.2 2.0 copy.74
  210.3 2.5 copy.64
  212.8 76.4 %all-to-all-done.1 = bf16[64,24,2048]{2,1,0:T(8,128)(2,1)} async-done(((bf16[64,24,2048]{2,1,0:T(8,128)(2,1)}), bf16[64,24,2048]{2,1,0:T(8,128)(2,1)}, u32[]{:S(2)}, u32[]{:S(2)}) %all-to-all-start.1) | async-done | bytes 6291488 | tf_op jit(solution)/shard_map/all_to_all | solution.py:81
  289.2 12.5 %gather_fusion.3 = bf16[1024,2048]{1,0:T(8,128)(2,1)} fusion(bf16[1536,2048]{1,0:T(8,128)(2,1)} %bitcast.10, s32[1024]{0:T(1024)S(1)} %broadcast_clamp_fusion), kind=kCustom, calls=%fused_computation.3 | custom fusion | bytes 8392704 | tf_op jit(solution)/shard_map/gather | solution.py:86
  301.6 6.6 %fusion.14 = f32[128,2048]{1,0:T(8,128)S(1)} fusion(bf16[1024,2048]{1,0:T(8,128)(2,1)} %gather_fusion.3, f32[128,8]{1,0:T(8,128)S(1)} %copy.63), kind=kLoop, calls=%fused_computation.27 | loop fusion | flops 6029312 | bytes 5246976 | tf_op jit(solution)/shard_map/reduce_sum | solution.py:90
  309.5 5.3 stack.27
  314.8 8.1 %all-to-all-start.2 = ((bf16[64,128,2,256]{1,3,2,0:T(8,128)(2,1)}), bf16[64,128,2,256]{1,3,2,0:T(8,128)(2,1)}, u32[]{:S(2)}, u32[]{:S(2)}) async-start(bf16[64,128,2,256]{1,3,2,0:T(8,128)(2,1)} %stack.27), calls=%async_computation.2 | async-start | bytes 16777216 | tf_op jit(solution)/shard_map/all_to_all | solution.py:123
  322.9 4.7 fusion.29
  329.2 102.4 %all-to-all-done.2 = bf16[64,128,2,256]{1,3,2,0:T(8,128)(2,1)} async-done(((bf16[64,128,2,256]{1,3,2,0:T(8,128)(2,1)}), bf16[64,128,2,256]{1,3,2,0:T(8,128)(2,1)}, u32[]{:S(2)}, u32[]{:S(2)}) %all-to-all-start.2) | async-done | bytes 8388640 | tf_op jit(solution)/shard_map/all_to_all | solution.py:123
  431.6 12.0 %copy.65 = bf16[64,128,2,256]{1,0,3,2:T(8,128)(2,1)} copy(bf16[64,128,2,256]{1,3,2,0:T(8,128)(2,1)} %all-to-all-done.2) | data formatting | bytes 16777216 | tf_op jit(solution)/shard_map/all_to_all | solution.py:123
  443.6 13.3 %reshape_reshape.3 = bf16[8,1024,2,2,128]{1,0,4,3,2:T(8,128)(2,1)} reshape(bf16[64,128,2,256]{1,0,3,2:T(8,128)(2,1)} %copy.65) | data formatting | bytes 16777216 | tf_op jit(solution)/shard_map/reshape;reshape | solution.py:127
  456.9 12.0 %copy.69 = bf16[8,1024,2,2,128]{4,1,3,2,0:T(8,128)(2,1)} copy(bf16[8,1024,2,2,128]{1,0,4,3,2:T(8,128)(2,1)} %reshape_reshape.3) | data formatting | bytes 16777216
  468.9 111.7 %while.15 = (s32[]{:T(128)}, f32[2,1024]{1,0:T(2,128)S(1)}, f32[2,1024]{1,0:T(2,128)S(1)}, f32[2,1024,128]{2,1,0:T(8,128)S(1)}, bf16[8,1024,2,2,128]{4,1,3,2,0:T...) while((s32[]{:T(128)}, f32[2,1024]{1,0:T(2,128)S(1)}, ...), condition=%wide.region_14.15_spmd.clone, body=%wide.region_11.14_spmd.clone.sunk | while | flops 1091315712 | bytes 64618624 | solution.py:149
  468.9 1.3 dynamic-slice_bitcast_fusion.2
  470.2 4.5 bitcast_reduce_fusion.2
  474.7 4.9 fusion.42
  480.4 2.4 fusion.44
  482.9 1.3 dynamic-slice_bitcast_fusion.2
  484.2 4.5 bitcast_reduce_fusion.2
  488.7 4.9 fusion.42
  494.4 2.4 fusion.44
  496.8 1.3 dynamic-slice_bitcast_fusion.2
  498.1 4.5 bitcast_reduce_fusion.2
  502.6 4.9 fusion.42
  508.4 2.4 fusion.44
  510.8 1.3 dynamic-slice_bitcast_fusion.2
  512.1 4.5 bitcast_reduce_fusion.2
  516.6 4.9 fusion.42
  522.3 2.4 fusion.44
  524.8 1.3 dynamic-slice_bitcast_fusion.2
  526.1 4.5 bitcast_reduce_fusion.2
  530.6 4.9 fusion.42
  536.3 2.4 fusion.44
  538.7 1.3 dynamic-slice_bitcast_fusion.2
  540.0 4.5 bitcast_reduce_fusion.2
  544.5 4.9 fusion.42
  550.3 2.4 fusion.44
  552.7 1.3 dynamic-slice_bitcast_fusion.2
  554.0 4.5 bitcast_reduce_fusion.2
  558.5 4.9 fusion.42
  564.3 2.4 fusion.44
  566.7 1.3 dynamic-slice_bitcast_fusion.2
  568.0 4.5 bitcast_reduce_fusion.2
  572.5 4.9 fusion.42
  578.2 2.4 fusion.44
  581.3 0.9 copy.80
  (108 shorter events, 14.2 us)
Async XLA Ops:
  33.7 11.9 %copy-start.5 = (s32[8192]{0:T(1024)S(1)}, s32[8192]{0:T(1024)}, u32[]{:S(2)}) copy-start(s32[8192]{0:T(1024)} %param.14) | copy-start | bytes 98308
  33.7 91.6 %all-to-all-start = ((bf16[64,24,2048]{2,1,0:T(8,128)(2,1)}), bf16[64,24,2048]{2,1,0:T(8,128)(2,1)}, u32[]{:S(2)}, u32[]{:S(2)}) async-start(bf16[64,24,2048]{2,1,0:T(8,128)(2,1)} %bitcast.106), calls=%async_computation | async-start | bytes 12582912 | tf_op jit(solution)/shard_map/all_to_all | solution.py:75
  172.4 19.4 %collective-permute-start = (f32[64,24,2048]{2,1,0:T(8,128)}, f32[64,24,2048]{2,1,0:T(8,128)S(1)}, u32[]{:S(2)}, u32[]{:S(2)}) collective-permute-start(f32[64,24,2048]{2,1,0:T(8,128)} %gather_fusion.2), channel_id=1, source_target_pairs={{0,1},{1,0},{2,3},{3,2},{4,5},{5,4},{6,7},{7,6},{8,9},{9,8},{10,11... | collective-permute-start | bytes 37748744 | tf_op jit(solution)/shard_map/ppermute | solution.py:17
  200.3 7.9 %copy-start.6 = (f32[128,8]{0,1:T(8,128)S(1)}, f32[128,8]{0,1:T(8,128)}, u32[]{:S(2)}) copy-start(f32[128,8]{0,1:T(8,128)} %param.16) | copy-start | bytes 12292
  200.3 88.9 %all-to-all-start.1 = ((bf16[64,24,2048]{2,1,0:T(8,128)(2,1)}), bf16[64,24,2048]{2,1,0:T(8,128)(2,1)}, u32[]{:S(2)}, u32[]{:S(2)}) async-start(bf16[64,24,2048]{2,1,0:T(8,128)(2,1)} %add_convert_fusion), calls=%async_computation.1 | async-start | bytes 12582912 | tf_op jit(solution)/shard_map/all_to_all | solution.py:81
  289.2 19.1 %copy-start.3 = (bf16[128,2048]{1,0:T(8,128)(2,1)S(1)}, bf16[128,2048]{1,0:T(8,128)(2,1)}, u32[]{:S(2)}) copy-start(bf16[128,2048]{1,0:T(8,128)(2,1)} %param.13) | copy-start | bytes 1572868
  301.6 6.9 %copy-start.2 = (bf16[512,2048]{1,0:T(8,128)(2,1)S(1)}, bf16[512,2048]{1,0:T(8,128)(2,1)}, u32[]{:S(2)}) copy-start(bf16[512,2048]{1,0:T(8,128)(2,1)} %copy.64) | copy-start | bytes 6291460
  301.6 6.9 %copy-start.4 = (f32[2048]{0:T(1024)S(1)}, f32[2048]{0:T(1024)}, u32[]{:S(2)}) copy-start(f32[2048]{0:T(1024)} %param.19) | copy-start | bytes 24580
  301.6 7.8 %copy-start.8 = (f32[128]{0:T(128)S(1)}, f32[128]{0:T(128)}, u32[]{:S(2)}) copy-start(f32[128]{0:T(128)} %param.23) | copy-start | bytes 1540
  308.5 14.4 %copy-start.1 = (f32[128,2048]{1,0:T(8,128)}, f32[128,2048]{1,0:T(8,128)S(1)}, u32[]{:S(2)}) copy-start(f32[128,2048]{1,0:T(8,128)S(1)} %get-tuple-element.109) | copy-start | bytes 3145732
  314.8 116.8 %all-to-all-start.2 = ((bf16[64,128,2,256]{1,3,2,0:T(8,128)(2,1)}), bf16[64,128,2,256]{1,3,2,0:T(8,128)(2,1)}, u32[]{:S(2)}, u32[]{:S(2)}) async-start(bf16[64,128,2,256]{1,3,2,0:T(8,128)(2,1)} %stack.27), calls=%async_computation.2 | async-start | bytes 16777216 | tf_op jit(solution)/shard_map/all_to_all | solution.py:123
  327.6 1.1 copy-start.7
  474.7 5.8 copy-start
  488.6 5.8 copy-start
  502.6 5.8 copy-start
  516.6 5.8 copy-start
  530.5 5.8 copy-start
  544.5 5.8 copy-start
  558.5 5.8 copy-start
  572.4 5.8 copy-start
